TPU v7x, 512 devices: a whole 4x4x16 slice. The times are simulated.
512 devices in a mesh: front: 128 (over x, z, core), chain: 4 (over y).
Axes of the slice: x: 4, y: 4, z: 16, core: 2. Of those that a mesh axis runs over, the one named last changes fastest.
Arguments:
- rhs: float32 [131072, 128], P(('front', 'chain')), may hold values from -6 to 6
- child_blocks: bfloat16 [45056, 128, 128], P(('front', 'chain')), may hold values from -4 to 4
- dest_front: int32 [45056, 1], P(('front', 'chain')), may hold values from 0 to 127; in each aligned block of 88 rows (0 to 87, 88 to 175, ...) at most 2 rows name the same one
- dest_place: int32 [45056], P(('front', 'chain')), may hold values from -4 to 23
- front_pivots: int32 [128], P('front'), may hold values from 512 to 1024, as said below
- diag_inv: float32 [131072, 256], P(('front', 'chain')), as said below
- lower_factor: bfloat16 [131072, 768], P(('front', 'chain')), may hold values from -0.1875 to 0.1875
- update_factor: bfloat16 [262144, 1024], P(('front', 'chain')), may hold values from -0.1875 to 0.1875
Outputs:
- solution: float32 [131072, 128], P(('front', 'chain'))
- update_out: float32 [262144, 128], P(('front', 'chain'))
Inputs may be any that keep to these rules, and one draw needn't show every extreme that they name: `dest_front`: at most 2 of the 88 blocks of one device go to one front, and that many do in every draw. `front_pivots`: pivot rows at or beyond this count are padding and solve to zero; some front has all 1024. `diag_inv`: each 256 by 256 block is lower triangular with its diagonal between 0.4 and 1.6.
All inputs are finite; a program needn't handle non-finite values.
Results may differ from a plain program's by a relative error of at most 0.0027.
Values may be sent and summed in bfloat16 or wider, within the bound.
No kernel may reach another device: no remote copies, remote signals or barrier semaphores. Data moves between devices by JAX's collectives and lax.ppermute only.
A program may use at most 64 MiB of HBM per device.

v0:
```python
import jax
import jax.numpy as jnp
from jax import lax
from jax.sharding import PartitionSpec as P

BR = 128


def broadcast(value, axis, source):
    kept = jnp.where(lax.axis_index(axis) == source, value, 0).astype(value.dtype)
    return lax.psum(kept, axis)


def slot_table(blocks, fronts, places, dest_count, slot_width):
    block_count = fronts.shape[0]
    sequence = jnp.arange(block_count, dtype=jnp.int32)
    earlier = (fronts[None, :] == fronts[:, None]) & (sequence[None, :] < sequence[:, None])
    rank_of = jnp.sum(earlier.astype(jnp.int32), axis=1)
    target = fronts * slot_width + rank_of
    source = jnp.full((dest_count * slot_width,), block_count, jnp.int32).at[target].set(sequence)
    slot_data = jnp.take(blocks, source, axis=0, mode="fill", fill_value=0)
    labels = jnp.take(places, source, axis=0, mode="fill", fill_value=-1)
    return (
        slot_data.reshape((dest_count, slot_width) + blocks.shape[1:]),
        labels.reshape(dest_count, slot_width),
    )


def assemble(slot_data, labels, piv_blocks, upd_blocks, owners):
    flattened = slot_data.reshape((-1,) + slot_data.shape[2:])
    tag_list = labels.reshape(-1)
    per_owner = piv_blocks + upd_blocks
    first_update = piv_blocks * owners
    update_index = tag_list - first_update
    placed = jnp.where(
        tag_list < first_update,
        tag_list // piv_blocks * per_owner + tag_list % piv_blocks,
        update_index // upd_blocks * per_owner + piv_blocks + update_index % upd_blocks,
    )
    placed = jnp.where(tag_list < 0, -1, placed)
    row_ids = jnp.arange(owners * per_owner, dtype=jnp.int32)
    onehot = (placed[None, :] == row_ids[:, None]).astype(jnp.bfloat16)
    return jnp.einsum("km,mrs->krs", onehot, flattened, preferred_element_type=jnp.float32)


def body(
    rhs, child_blocks, dest_front, dest_place, front_pivots, diag_inv, lower_factor, update_factor
):
    owners = lax.axis_size("chain")
    front_count = lax.axis_size("front")
    chain_at = lax.axis_index("chain")
    piv_rows = rhs.shape[0]
    upd_rows = update_factor.shape[0]
    source_width = rhs.shape[1]
    piv_blocks = piv_rows // BR
    upd_blocks = upd_rows // BR
    per_device = child_blocks.shape[0]
    capacity = max(2, (per_device + front_count - 1) // front_count * 2)
    slot_data, labels = slot_table(
        child_blocks, dest_front[:, 0], dest_place, front_count, capacity
    )
    received, received_labels = (
        lax.all_to_all(slot_data, "front", split_axis=0, concat_axis=0, tiled=True),
        lax.all_to_all(labels, "front", split_axis=0, concat_axis=0, tiled=True),
    )
    merged = assemble(received, received_labels, piv_blocks, upd_blocks, owners)
    owned = lax.psum_scatter(merged, "chain", scatter_dimension=0, tiled=True)
    pivot_rhs = rhs + owned[:piv_blocks].reshape(piv_rows, source_width)
    update_start = owned[piv_blocks:].reshape(upd_rows, source_width)
    positions = chain_at * piv_rows + jnp.arange(piv_rows, dtype=jnp.int32)
    live_rows = (positions < front_pivots[0]).astype(jnp.float32)[:, None]
    running = pivot_rhs
    updates = update_start
    solved = jnp.zeros_like(pivot_rhs)
    for section in range(owners):
        candidate = live_rows * jnp.dot(diag_inv, running, precision=lax.Precision.HIGHEST)
        solved = jnp.where(chain_at == section, candidate, solved)
        solved_bf = broadcast(candidate.astype(jnp.bfloat16), "chain", section)
        advance_running = running
        advance_updates = updates
        if section < owners - 1:
            factor_block = lower_factor[:, section * piv_rows : (section + 1) * piv_rows]
            product = jnp.dot(factor_block, solved_bf, preferred_element_type=jnp.float32)
            advance_running = advance_running - jnp.where(chain_at > section, product, 0.0)
        update_block = update_factor[:, section * piv_rows : (section + 1) * piv_rows]
        advance_updates = advance_updates - jnp.dot(
            update_block, solved_bf, preferred_element_type=jnp.float32
        )
        running = advance_running
        updates = advance_updates
    return (solved, updates)


def solution(mesh):
    return jax.shard_map(
        body,
        mesh=mesh,
        in_specs=(
            P(("front", "chain"), None),
            P(("front", "chain"), None, None),
            P(("front", "chain"), None),
            P(("front", "chain")),
            P("front"),
            P(("front", "chain"), None),
            P(("front", "chain"), None),
            P(("front", "chain"), None),
        ),
        out_specs=(P(("front", "chain"), None), P(("front", "chain"), None)),
        check_vma=False,
    )
```

profile of v0, /device:TPU:2, one launch (start us, length us, event | category | flops | bytes accessed | tf_op | source)
XLA Modules:
  0.0 734.5 jit_solution(3407166581159611724)
XLA Ops:
  9.7 1.9 gather_fusion
  12.4 19.5 %all-to-all-start = ((s32[128,1,2]{2,1,0:T(1,128)}), s32[128,1,2]{2,1,0:T(1,128)S(1)}, u32[]{:S(2)}, u32[]{:S(2)}) async-start(s32[128,1,2]{2,1,0:T(1,128)} %bitcast.4), calls=%async_computation | async-start | bytes 131072 | tf_op jit(solution)/shard_map/all_to_all | solution.py:64
  32.1 8.4 %gather_fusion.1 = bf16[256,128,128]{2,1,0:T(8,128)(2,1)} fusion(bf16[88,128,128]{2,1,0:T(8,128)(2,1)S(1)} %copy-done, s32[1024]{0:T(1024)S(1)} %pad_clamp_fusion), kind=kCustom, calls=%fused_computation.1 | custom fusion | bytes 16778240 | tf_op jit(solution)/shard_map/jit(_take)/gather | solution.py:21
  40.5 7.3 broadcast_select_fusion
  47.8 16.3 %copy.40 = bf16[128,2,128,128]{3,1,2,0:T(2,128)(2,1)} copy(bf16[128,2,128,128]{3,2,1,0:T(8,128)(2,1)} %broadcast_select_fusion) | data formatting | bytes 16777216 | tf_op jit(solution)/shard_map/jit(_take)/select_n | solution.py:21
  64.1 16.7 %all-to-all-start.1 = ((bf16[128,2,128,128]{3,1,2,0:T(2,128)(2,1)}), bf16[128,2,128,128]{3,1,2,0:T(2,128)(2,1)}, u32[]{:S(2)}, u32[]{:S(2)}) async-start(bf16[128,2,128,128]{3,1,2,0:T(2,128)(2,1)} %copy.40), calls=%async_computation.1 | async-start | bytes 16777216 | tf_op jit(solution)/shard_map/all_to_all | solution.py:63
  82.3 364.7 %all-to-all-done.1 = bf16[128,2,128,128]{3,1,2,0:T(2,128)(2,1)} async-done(((bf16[128,2,128,128]{3,1,2,0:T(2,128)(2,1)}), bf16[128,2,128,128]{3,1,2,0:T(2,128)(2,1)}, u32[]{:S(2)}, u32[]{:S(2)}) %all-to-all-start.1) | async-done | bytes 8388640 | tf_op jit(solution)/shard_map/all_to_all | solution.py:63
  447.0 7.3 copy.41
  454.4 1.2 fusion.19
  455.5 1.5 copy.42
  458.0 28.3 %reduce-scatter.2.cloned.1.call-done = f32[6,128,128]{2,1,0:T(8,128)} async-done(((f32[24,128,128]{2,1,0:T(8,128)}), f32[6,128,128]{2,1,0:T(8,128)}) %reduce-scatter.2.cloned.1.call-update) | async-done | bytes 393232 | tf_op jit(solution)/shard_map/reduce_scatter | solution.py:67
  488.5 1.7 slice.41
  490.2 1.8 copy.45
  492.0 53.7 %all-reduce.5.cloned.1.call-done = bf16[256,128]{0,1:T(8,128)(2,1)} async-done(((bf16[256,128]{0,1:T(8,128)(2,1)}), bf16[256,128]{0,1:T(8,128)(2,1)}) %all-reduce.5.cloned.1.call-update) | async-done | bytes 65552 | tf_op jit(solution)/shard_map/psum | solution.py:11
  545.7 1.1 fusion.9
  547.9 2.0 fusion.3
  549.9 55.7 %all-reduce.7.cloned.1.call-done = bf16[256,128]{0,1:T(8,128)(2,1)} async-done(((bf16[256,128]{0,1:T(8,128)(2,1)}), bf16[256,128]{0,1:T(8,128)(2,1)}) %all-reduce.7.cloned.1.call-update) | async-done | bytes 65552 | tf_op jit(solution)/shard_map/psum | solution.py:11
  608.6 2.0 fusion.2
  610.6 55.2 %all-reduce.9.cloned.1.call-done = bf16[256,128]{0,1:T(8,128)(2,1)} async-done(((bf16[256,128]{0,1:T(8,128)(2,1)}), bf16[256,128]{0,1:T(8,128)(2,1)}) %all-reduce.9.cloned.1.call-update) | async-done | bytes 65552 | tf_op jit(solution)/shard_map/psum | solution.py:11
  665.7 1.2 fusion.5
  668.7 1.3 fusion.1
  670.7 1.7 copy.46
  672.3 53.6 %all-reduce.11.cloned.1.call-done = bf16[256,128]{0,1:T(8,128)(2,1)} async-done(((bf16[256,128]{0,1:T(8,128)(2,1)}), bf16[256,128]{0,1:T(8,128)(2,1)}) %all-reduce.11.cloned.1.call-update) | async-done | bytes 65552 | tf_op jit(solution)/shard_map/psum | solution.py:11
  725.9 1.2 fusion
  (50 shorter events, 14.7 us)
Async XLA Ops:
  7.2 25.0 %copy-start = (bf16[88,128,128]{2,1,0:T(8,128)(2,1)S(1)}, bf16[88,128,128]{2,1,0:T(8,128)(2,1)}, u32[]{:S(2)}) copy-start(bf16[88,128,128]{2,1,0:T(8,128)(2,1)} %param.9) | copy-start | bytes 8650756
  12.4 51.7 %all-to-all-start = ((s32[128,1,2]{2,1,0:T(1,128)}), s32[128,1,2]{2,1,0:T(1,128)S(1)}, u32[]{:S(2)}, u32[]{:S(2)}) async-start(s32[128,1,2]{2,1,0:T(1,128)} %bitcast.4), calls=%async_computation | async-start | bytes 131072 | tf_op jit(solution)/shard_map/all_to_all | solution.py:64
  64.1 382.9 %all-to-all-start.1 = ((bf16[128,2,128,128]{3,1,2,0:T(2,128)(2,1)}), bf16[128,2,128,128]{3,1,2,0:T(2,128)(2,1)}, u32[]{:S(2)}, u32[]{:S(2)}) async-start(bf16[128,2,128,128]{3,1,2,0:T(2,128)(2,1)} %copy.40), calls=%async_computation.1 | async-start | bytes 16777216 | tf_op jit(solution)/shard_map/all_to_all | solution.py:63
  80.8 405.6 %reduce-scatter.2.cloned.1.call-start = ((), (), s32[]{:S(2)}) async-start(), calls=%async_computation.3 | async-start | bytes 1966080 | tf_op jit(solution)/shard_map/reduce_scatter | solution.py:67
  454.3 2.9 copy-start.4
  454.3 33.1 %copy-start.1 = (f32[256,256]{1,0:T(8,128)S(1)}, f32[256,256]{1,0:T(8,128)}, u32[]{:S(2)}) copy-start(f32[256,256]{1,0:T(8,128)} %param.13) | copy-start | bytes 786436
  457.0 88.6 %all-reduce.5.cloned.1.call-start = ((), (), s32[]{:S(2)}) async-start(), calls=%async_computation.4 | async-start | bytes 131072 | tf_op jit(solution)/shard_map/psum | solution.py:11
  488.5 117.2 %all-reduce.7.cloned.1.call-start = ((), (), s32[]{:S(2)}) async-start(), calls=%async_computation.5 | async-start | bytes 131072 | tf_op jit(solution)/shard_map/psum | solution.py:11
  547.9 117.8 %all-reduce.9.cloned.1.call-start = ((), (), s32[]{:S(2)}) async-start(), calls=%async_computation.6 | async-start | bytes 131072 | tf_op jit(solution)/shard_map/psum | solution.py:11
  606.8 0.7 copy-start.3
  608.5 117.4 %all-reduce.11.cloned.1.call-start = ((), (), s32[]{:S(2)}) async-start(), calls=%async_computation.7 | async-start | bytes 131072 | tf_op jit(solution)/shard_map/psum | solution.py:11
  667.3 0.7 copy-start.2
Sparse Core Ops, SparseCore 0:
  457.2 29.1 reduce-scatter.1
  489.2 56.3 all-reduce.4
  548.6 57.0 all-reduce.6
  608.6 57.0 all-reduce.8
  668.8 57.0 all-reduce.10
where the time goes:
time: 735 us; the launch traced here: 734 us
  waiting for transfers between devices  611 us (83%)
  local copies, waits for them, and re-layouts  46.1 us (6%)
  starting transfers between devices  36.6 us (5%)
  between operations  14.7 us (2%)
  other arithmetic  13.1 us (2%)
  matrix products  12.8 us (2%)
    all_to_all x1, waiting for transfers between devices, body(): lax.all_to_all(slot_data, 'front', split_axis=0, concat_axis=0, tiled=True)  365 us
    psum x4, waiting for transfers between devices, broadcast(): return lax.psum(kept, axis)  218 us
    reduce_scatter x1, waiting for transfers between devices, body(): owned = lax.psum_scatter(merged, 'chain', scatter_dimension=0, tiled=True)  28.3 us
    all_to_all x1, starting transfers between devices, body(): lax.all_to_all(labels, 'front', split_axis=0, concat_axis=0, tiled=True)  19.5 us
    all_to_all x1, starting transfers between devices, body(): lax.all_to_all(slot_data, 'front', split_axis=0, concat_axis=0, tiled=True)  16.7 us
    select_n x1, local copies, waits for them, and re-layouts, slot_table(): slot_data = jnp.take(blocks, source, axis=0, mode='fill', fill_value=0)  16.3 us
  transfers between devices with their start and end apart: 7, of which 6 were waited for; matrix products, arithmetic and copies ran while one was open for 6% of the time, Pallas kernels for 0%

commit v1 on v0

--- a/solution.py
+++ b/solution.py
@@ -8,7 +8,7 @@
 
 def broadcast(value, axis, source):
     kept = jnp.where(lax.axis_index(axis) == source, value, 0).astype(value.dtype)
-    return lax.psum(kept, axis)
+    return jnp.sum(lax.all_gather(kept, axis), axis=0)
 
 
 def slot_table(blocks, fronts, places, dest_count, slot_width):

time: 735 us -> 575 us (0.78)
  waiting for transfers between devices: 611 us -> 393 us
  blocking collectives: 0 us -> 51.7 us
    psum x4 -> x0, waiting for transfers between devices: 218 us -> none  [broadcast(): return lax.psum(kept, axis)]
    all_gather x0 -> x4, blocking collectives: none -> 51.7 us  [broadcast(): return jnp.sum(lax.all_gather(kept, axis), axis=0)]
  transfers between devices with their start and end apart: 7 -> 3, of which waited for: 6 -> 2; matrix products, arithmetic and copies ran while one was open for 6% -> 6% of each run, Pallas kernels for 0% -> 0%
where the time goes in v1:
time: 575 us; the launch traced here: 574 us
  waiting for transfers between devices  393 us (68%)
  blocking collectives  51.7 us (9%)
  local copies, waits for them, and re-layouts  48.8 us (8%)
  starting transfers between devices  36.4 us (6%)
  other arithmetic  17.1 us (3%)
  between operations  15 us (3%)
  matrix products  11.9 us (2%)
    all_to_all x1, waiting for transfers between devices, body(): lax.all_to_all(slot_data, 'front', split_axis=0, concat_axis=0, tiled=True)  365 us
    all_gather x4, blocking collectives, broadcast(): return jnp.sum(lax.all_gather(kept, axis), axis=0)  51.7 us
    reduce_scatter x1, waiting for transfers between devices, body(): owned = lax.psum_scatter(merged, 'chain', scatter_dimension=0, tiled=True)  28.5 us
    all_to_all x1, starting transfers between devices, body(): lax.all_to_all(labels, 'front', split_axis=0, concat_axis=0, tiled=True)  19.5 us
    all_to_all x1, starting transfers between devices, body(): lax.all_to_all(slot_data, 'front', split_axis=0, concat_axis=0, tiled=True)  16.7 us
    select_n x1, local copies, waits for them, and re-layouts, slot_table(): slot_data = jnp.take(blocks, source, axis=0, mode='fill', fill_value=0)  16.3 us
  transfers between devices with their start and end apart: 3, of which 2 were waited for; matrix products, arithmetic and copies ran while one was open for 6% of the time, Pallas kernels for 0%

profile of v1, /device:TPU:2, one launch (start us, length us, event | category | flops | bytes accessed | tf_op | source)
XLA Modules:
  0.0 574.0 jit_solution(17042543165254643444)
XLA Ops:
  9.7 1.9 gather_fusion
  12.4 19.5 %all-to-all-start = ((s32[128,1,2]{2,1,0:T(1,128)}), s32[128,1,2]{2,1,0:T(1,128)S(1)}, u32[]{:S(2)}, u32[]{:S(2)}) async-start(s32[128,1,2]{2,1,0:T(1,128)} %bitcast.4), calls=%async_computation | async-start | bytes 131072 | tf_op jit(solution)/shard_map/all_to_all | solution.py:64
  32.1 8.4 %gather_fusion.1 = bf16[256,128,128]{2,1,0:T(8,128)(2,1)} fusion(bf16[88,128,128]{2,1,0:T(8,128)(2,1)S(1)} %copy-done, s32[1024]{0:T(1024)S(1)} %pad_clamp_fusion), kind=kCustom, calls=%fused_computation.1 | custom fusion | bytes 16778240 | tf_op jit(solution)/shard_map/jit(_take)/gather | solution.py:21
  40.5 7.3 %broadcast_select_fusion = bf16[128,2,128,128]{3,2,1,0:T(8,128)(2,1)} fusion(bf16[128,2,128,128]{3,2,1,0:T(8,128)(2,1)} %bitcast.79, pred[128,2]{1,0:T(8,128)(4,1)S(1)} %broadcast_in_dim.50), kind=kLoop, calls=%fused_computation.3 | loop fusion | flops 4194304 | bytes 16777472 | tf_op jit(solution)/shard_map/jit(_take)/select_n | solution.py:21
  47.8 16.3 %copy.40 = bf16[128,2,128,128]{3,1,2,0:T(2,128)(2,1)} copy(bf16[128,2,128,128]{3,2,1,0:T(8,128)(2,1)} %broadcast_select_fusion) | data formatting | bytes 16777216 | tf_op jit(solution)/shard_map/jit(_take)/select_n | solution.py:21
  64.0 16.7 %all-to-all-start.1 = ((bf16[128,2,128,128]{3,1,2,0:T(2,128)(2,1)}), bf16[128,2,128,128]{3,1,2,0:T(2,128)(2,1)}, u32[]{:S(2)}, u32[]{:S(2)}) async-start(bf16[128,2,128,128]{3,1,2,0:T(2,128)(2,1)} %copy.40), calls=%async_computation.1 | async-start | bytes 16777216 | tf_op jit(solution)/shard_map/all_to_all | solution.py:63
  82.4 364.5 %all-to-all-done.1 = bf16[128,2,128,128]{3,1,2,0:T(2,128)(2,1)} async-done(((bf16[128,2,128,128]{3,1,2,0:T(2,128)(2,1)}), bf16[128,2,128,128]{3,1,2,0:T(2,128)(2,1)}, u32[]{:S(2)}, u32[]{:S(2)}) %all-to-all-start.1) | async-done | bytes 8388640 | tf_op jit(solution)/shard_map/all_to_all | solution.py:63
  447.0 7.3 %copy.41 = bf16[128,2,128,128]{3,1,0,2:T(2,128)(2,1)S(1)} copy(bf16[128,2,128,128]{3,1,2,0:T(2,128)(2,1)} %all-to-all-done.1) | data formatting | bytes 16777216 | tf_op jit(solution)/shard_map/all_to_all | solution.py:63
  455.5 1.4 copy.42
  457.8 28.5 %reduce-scatter.2.cloned.1.call-done = f32[6,128,128]{2,1,0:T(8,128)} async-done(((f32[24,128,128]{2,1,0:T(8,128)}), f32[6,128,128]{2,1,0:T(8,128)}) %reduce-scatter.2.cloned.1.call-update) | async-done | bytes 393232 | tf_op jit(solution)/shard_map/reduce_scatter | solution.py:67
  487.8 13.2 %all-gather = bf16[1024,128]{0,1:T(8,128)(2,1)} all-gather(bf16[256,128]{0,1:T(8,128)(2,1)S(1)} %select_bitcast_fusion.4), channel_id=2, replica_groups=mesh['front'=128,'chain'=4] {'chain'}, dimensions={0}, use_global_device_ids=true | all-gather | bytes 327680 | tf_op jit(solution)/shard_map/all_gather | solution.py:11
  501.0 1.8 reshape.176
  502.9 1.9 reduce_sum.61
  506.3 13.0 %all-gather.1 = bf16[1024,128]{0,1:T(8,128)(2,1)} all-gather(bf16[256,128]{0,1:T(8,128)(2,1)S(1)} %select_bitcast_fusion.3), channel_id=3, replica_groups=mesh['front'=128,'chain'=4] {'chain'}, dimensions={0}, use_global_device_ids=true | all-gather | bytes 327680 | tf_op jit(solution)/shard_map/all_gather | solution.py:11
  519.3 1.8 reshape.177
  521.2 1.9 reduce_sum.62
  525.3 13.0 %all-gather.2 = bf16[1024,128]{0,1:T(8,128)(2,1)} all-gather(bf16[256,128]{0,1:T(8,128)(2,1)S(1)} %select_bitcast_fusion.2), channel_id=4, replica_groups=mesh['front'=128,'chain'=4] {'chain'}, dimensions={0}, use_global_device_ids=true | all-gather | bytes 327680 | tf_op jit(solution)/shard_map/all_gather | solution.py:11
  538.3 1.8 reshape.178
  540.1 1.9 reduce_sum.63
  547.3 1.2 fusion.2
  548.5 1.9 fusion.1
  550.4 12.5 %all-gather.3 = bf16[1024,128]{0,1:T(8,128)(2,1)S(1)} all-gather(bf16[256,128]{0,1:T(8,128)(2,1)} %select_bitcast_fusion.1), channel_id=5, replica_groups=mesh['front'=128,'chain'=4] {'chain'}, dimensions={0}, use_global_device_ids=true | all-gather | bytes 327680 | tf_op jit(solution)/shard_map/all_gather | solution.py:11
  563.4 1.3 fusion
  565.5 1.7 copy.46
  (48 shorter events, 18.3 us)
Async XLA Ops:
  7.2 25.0 %copy-start = (bf16[88,128,128]{2,1,0:T(8,128)(2,1)S(1)}, bf16[88,128,128]{2,1,0:T(8,128)(2,1)}, u32[]{:S(2)}) copy-start(bf16[88,128,128]{2,1,0:T(8,128)(2,1)} %param.9) | copy-start | bytes 8650756
  12.4 51.6 %all-to-all-start = ((s32[128,1,2]{2,1,0:T(1,128)}), s32[128,1,2]{2,1,0:T(1,128)S(1)}, u32[]{:S(2)}, u32[]{:S(2)}) async-start(s32[128,1,2]{2,1,0:T(1,128)} %bitcast.4), calls=%async_computation | async-start | bytes 131072 | tf_op jit(solution)/shard_map/all_to_all | solution.py:64
  64.0 382.9 %all-to-all-start.1 = ((bf16[128,2,128,128]{3,1,2,0:T(2,128)(2,1)}), bf16[128,2,128,128]{3,1,2,0:T(2,128)(2,1)}, u32[]{:S(2)}, u32[]{:S(2)}) async-start(bf16[128,2,128,128]{3,1,2,0:T(2,128)(2,1)} %copy.40), calls=%async_computation.1 | async-start | bytes 16777216 | tf_op jit(solution)/shard_map/all_to_all | solution.py:63
  80.7 405.6 %reduce-scatter.2.cloned.1.call-start = ((), (), s32[]{:S(2)}) async-start(), calls=%async_computation.3 | async-start | bytes 1966080 | tf_op jit(solution)/shard_map/reduce_scatter | solution.py:67
  454.3 2.7 copy-start.3
  454.3 33.0 %copy-start.1 = (f32[256,256]{1,0:T(8,128)S(1)}, f32[256,256]{1,0:T(8,128)}, u32[]{:S(2)}) copy-start(f32[256,256]{1,0:T(8,128)} %param.13) | copy-start | bytes 786436
  524.2 0.7 copy-start.2
Sparse Core Ops, SparseCore 0:
  457.1 29.1 reduce-scatter.1
